TPU v7x, 32 devices: a whole 2x2x4 slice. The times are simulated.
32 devices in a mesh: groups: 2 (over x), exp: 16 (over z, y, core).
Axes of the slice: x: 2, y: 2, z: 4, core: 2. Of those that a mesh axis runs over, the one named last changes fastest.
Arguments:
- estimate: float32 [512, 4, 512], P('exp', 'groups'), parts along dimension 1, may hold values from -6 to 6
- observed: bfloat16 [32, 512, 512], P(('groups', 'exp')), parts along dimension 0, may hold values from -12 to 12
- pixel_mask: int32 [32, 512, 512], P(('groups', 'exp')), parts along dimension 0, may hold values 0 or 1
- blur_mix: float32 [32, 6, 8, 8], P(('groups', 'exp')), parts along dimension 0, may hold values from 0.2 to 1
- dithers: int32 [32, 2], P(('groups', 'exp')), parts along dimension 0, may hold values from -8 to 8, as said below
- patch_of: int32 [32], P(('groups', 'exp')), parts along dimension 0, may hold values from 0 to 1
- column_taps: bfloat16 [6, 15], replicated, may hold values from 0 to 0.119628906
- row_taps: bfloat16 [6, 15], replicated, may hold values from 0 to 0.119628906
Outputs:
- gradient: float32 [512, 4, 512], P('exp', 'groups'), parts along dimension 1
There are 2 independent parts, one for each index of `groups`. A program takes and returns all parts, laid end to end along the dimension named above; an argument that names none is the same for every part. Nothing has to cross between parts.
Inputs may be any that keep to these rules, and one draw needn't show every extreme that they name: `dithers`: each exposure's two offsets; the value 8 occurs among the row offsets and -8 among the column offsets.
All inputs are finite; a program needn't handle non-finite values. No bound on the sum of `pixel_mask` on one device may be relied on, other than what follows from the above.
Results may differ from a plain program's by a relative error of at most 0.004.
Values may be sent and summed in bfloat16 or wider, within the bound.
No kernel may reach another device: no remote copies, remote signals or barrier semaphores. Data moves between devices by JAX's collectives and lax.ppermute only.
A program may use at most 128 MiB of HBM per device.

v0:
```python
import jax
import jax.numpy as jnp
from jax import lax
from jax.sharding import PartitionSpec as P

DMAX = 8


def band_stack(tap_values, extent, col_offset):
    half_width = tap_values.shape[1] // 2
    source = lax.broadcasted_iota(jnp.int32, (extent, extent), 0)
    target = lax.broadcasted_iota(jnp.int32, (extent, extent), 1)
    offset = source - target - col_offset + half_width
    inside = (source - col_offset >= 0) & (source - col_offset < extent)
    running = jnp.zeros((tap_values.shape[0], extent, extent), jnp.float32)
    for tap_index in range(tap_values.shape[1]):
        matches = ((offset == tap_index) & inside).astype(jnp.float32)
        running = (
            running + tap_values[:, tap_index].astype(jnp.float32)[:, None, None] * matches[None]
        )
    return running.astype(jnp.bfloat16)


def exposure_back(rowed, frame_data, mask_frame, blur_weights, row_shift, column_band):
    extent = frame_data.shape[0]
    basis_count = blur_weights.shape[0]
    tile_count = blur_weights.shape[1]
    tile_side = extent // tile_count
    padded = jnp.pad(rowed, ((DMAX, DMAX), (0, 0)))
    shifted = lax.dynamic_slice_in_dim(padded, DMAX + row_shift, extent, 0).reshape(
        extent, basis_count, extent
    )
    blurred = jnp.einsum("kba,bkc->kac", column_band, shifted, preferred_element_type=jnp.float32)
    mix_full = jnp.broadcast_to(
        blur_weights[:, :, None, :, None],
        (basis_count, tile_count, tile_side, tile_count, tile_side),
    ).reshape(basis_count, extent, extent)
    model_image = jnp.sum(mix_full * blurred, axis=0)
    residual = mask_frame.astype(jnp.float32) * (model_image - frame_data.astype(jnp.float32))
    weighted = (mix_full * residual[None]).astype(jnp.bfloat16)
    backed = jnp.einsum("kab,kbc->akc", column_band, weighted, preferred_element_type=jnp.float32)
    backed = backed.astype(jnp.bfloat16).reshape(extent, basis_count * extent)
    return jnp.pad(backed, ((DMAX, DMAX), (0, 0)))


def back_rows(padded_back, back_stack, row_shift, patch_index, patch_count, first_row, row_count):
    picked = lax.dynamic_slice_in_dim(padded_back, first_row + DMAX - row_shift, row_count, 0)
    result = jnp.dot(picked, back_stack, preferred_element_type=jnp.float32)
    selector = lax.broadcasted_iota(jnp.int32, (1, patch_count, 1), 1) == patch_index
    return jnp.where(selector, result[:, None, :], jnp.zeros((), jnp.float32))


def per_device(estimate, observed, pixel_mask, blur_mix, dithers, patch_of, column_taps, row_taps):
    extent = observed.shape[1]
    patch_count = estimate.shape[1]
    band_rows = estimate.shape[0]
    row_shift = dithers[0, 0]
    column_shift = dithers[0, 1]
    patch_index = patch_of[0]
    column_band = band_stack(column_taps, extent, 0)
    row_band = band_stack(row_taps, extent, column_shift)
    forward_stack = jnp.transpose(row_band, (1, 0, 2)).reshape(extent, -1)
    back_stack = jnp.transpose(row_band, (0, 2, 1)).reshape(-1, extent)
    estimate_low = estimate.astype(jnp.bfloat16)
    gathered = lax.all_gather(estimate_low, "exp", axis=0, tiled=True)
    chosen = lax.dynamic_index_in_dim(gathered, patch_index, 1, keepdims=False)
    rowed = jnp.dot(chosen, forward_stack, preferred_element_type=jnp.float32).astype(jnp.bfloat16)
    padded_back = exposure_back(
        rowed, observed[0], pixel_mask[0], blur_mix[0], row_shift, column_band
    )
    complete = lax.psum(
        back_rows(padded_back, back_stack, row_shift, patch_index, patch_count, 0, extent), "exp"
    )
    return lax.dynamic_slice_in_dim(complete, lax.axis_index("exp") * band_rows, band_rows, 0)


def solution(mesh):
    in_specs = (
        P("exp", "groups", None),
        P(("groups", "exp"), None, None),
        P(("groups", "exp"), None, None),
        P(("groups", "exp"), None, None, None),
        P(("groups", "exp"), None),
        P(("groups", "exp")),
        P(),
        P(),
    )
    out_specs = P("exp", "groups", None)
    return jax.shard_map(
        per_device, mesh=mesh, in_specs=in_specs, out_specs=out_specs, check_vma=False
    )
```

profile of v0, /device:TPU:0, one launch (start us, length us, event | category | flops | bytes accessed | tf_op | source)
XLA Modules:
  0.0 287.0 jit_solution(5062200893745384783)
XLA Ops:
  10.3 7.4 %fusion.68 = (f32[512,512]{0,1:T(8,128)S(1)}, f32[512,512]{0,1:T(8,128)}, f32[512,512]{0,1:T(8,128)S(1)}, f32[512,512]{0,1:T(8,128)S(1)}, f32[512,512]{0,1:T(8,1...) fusion(s32[]{:T(128)} %bitcast.3, ...), kind=kLoop, calls=%fused_computation.95 | loop fusion | flops 25165824 | bytes 31457796 | tf_op jit(solution)/shard_map/convert_element_type | solution.py:17
  18.0 8.4 %add_convert_fusion = bf16[512,6,512]{0,2,1:T(8,128)(2,1)} fusion(f32[512,512]{0,1:T(8,128)S(1)} %get-tuple-element.51, f32[6]{0:T(128)S(1)} %get-tuple-element.33, f32[512,512]{0,1:T(8,128)S(1)} %get-tuple-element.52, f32[6]{0:T(128)S(1)} %get-tuple-element.34, f32[512,512]{0,1:T(8,128)S(1)} %get-tuple-element.53, f32[6]{0:T(128)S(1)} %get-tuple-element.21, ...), kind=kLoop, calls=%fused_computation.32 | loop fusion | flops 47185920 | bytes 18874728 | tf_op jit(solution)/shard_map/convert_element_type | solution.py:21
  26.4 7.0 %fusion.128 = (f32[512,512]{0,1:T(8,128)}, f32[512,512]{0,1:T(8,128)}, f32[512,512]{0,1:T(8,128)}, f32[512,512]{0,1:T(8,128)}, f32[512,512]{0,1:T(8,128)}, /*ind...) fusion(pred[512]{0:T(512)(128)(4,1)S(1)} %iota_compare_fusion), kind=kLoop, calls=%fused_computation.155 | loop fusion | flops 12320768 | bytes 15729152 | tf_op jit(solution)/shard_map/convert_element_type | solution.py:17
  38.8 2.6 copy.12
  41.4 2.5 copy.13
  44.0 2.6 copy.14
  46.5 2.5 copy.15
  51.6 2.6 copy.17
  54.1 2.5 copy.18
  56.7 2.6 copy.19
  61.8 2.5 copy.21
  64.3 2.6 copy.22
  66.9 2.6 copy.23
  69.5 2.5 copy.24
  72.0 2.5 copy.25
  74.5 5.4 %broadcast_in_dim.19 = f32[6,8,64,8,64]{4,3,2,1,0:T(8,128)} broadcast(f32[6,8,8]{2,1,0:T(8,128)S(1)} %bitcast.127), dimensions={0,1,3} | broadcast | bytes 6292992 | tf_op jit(solution)/shard_map/broadcast_in_dim | solution.py:34
  80.0 11.5 %reshape.1297 = f32[6,512,512]{2,1,0:T(8,128)} reshape(f32[6,8,64,8,64]{4,3,2,1,0:T(8,128)} %broadcast_in_dim.19) | data formatting | bytes 12582912 | tf_op jit(solution)/shard_map/reshape | solution.py:37
  91.5 2.5 copy.31
  94.1 2.6 copy.32
  101.7 2.6 copy.35
  104.3 2.6 copy.36
  106.8 2.6 copy.37
  117.0 2.6 copy.41
  119.6 2.5 copy.42
  125.3 12.8 %fusion.1 = bf16[3072,512]{1,0:T(8,128)(2,1)} fusion(f32[512,512]{1,0:T(8,128)S(1)} %copy.45, f32[3072]{0:T(1024)S(1)} %mul.935, f32[512,512]{1,0:T(8,128)S(1)} %copy.44, f32[3072]{0:T(1024)S(1)} %mul.929, f32[512,512]{1,0:T(8,128)} %copy.43, f32[3072]{0:T(1024)S(1)} %mul.923, f32[512,512]{1,0:T(8,128)} %copy.42, f32[3072]{0:T(1024)S(1)} %mul.917, ...), kind=kLoop, calls=%fused_computation.2 | loop fusion | flops 47185920 | bytes 19058688 | tf_op jit(solution)/shard_map/convert_element_type | solution.py:21
  138.5 10.5 %add_convert_fusion.1 = bf16[6,512,512]{2,1,0:T(8,128)(2,1)S(1)} fusion(f32[512,512]{1,0:T(8,128)} %copy.25, f32[6]{0:T(128)S(1)} %get-tuple-element.18, f32[512,512]{1,0:T(8,128)} %copy.24, f32[6]{0:T(128)S(1)} %get-tuple-element.19, f32[512,512]{1,0:T(8,128)} %copy.23, f32[6]{0:T(128)S(1)} %get-tuple-element.6, f32[512,512]{1,0:T(8,128)} %copy.22, ...), kind=kLoop, calls=%fused_computation.33 | loop fusion | flops 47185920 | bytes 18874728 | tf_op jit(solution)/shard_map/convert_element_type | solution.py:21
  149.1 3.9 %convolution_convert_fusion = bf16[512,3072]{1,0:T(8,128)(2,1)S(1)} fusion(bf16[512,3072]{0,1:T(8,128)(2,1)} %bitcast.125, bf16[512,2,512]{2,0,1:T(8,128)(2,1)} %all-gather.2.cloned.1.call-done, s32[]{:T(128)S(6)} %select_n.17), kind=kOutput, calls=%fused_computation.34 | convolution fusion | flops 1612185600 | bytes 6815748 | tf_op jit(solution)/shard_map/dot_general | solution.py:67
  155.5 4.7 %copy.27 = bf16[512,3072]{0,1:T(8,128)(2,1)} copy(bf16[512,3072]{1,0:T(8,128)(2,1)} %pad_dynamic-slice_fusion.1) | data formatting | bytes 6291456 | tf_op jit(solution)/shard_map/dynamic_slice | solution.py:30
  160.3 6.2 %multiply_reduce_fusion = f32[512,512]{1,0:T(8,128)S(1)} fusion(f32[6,512,512]{2,1,0:T(8,128)} %reshape.1297, bf16[6,512,512]{2,1,0:T(8,128)(2,1)S(1)} %add_convert_fusion.1, bf16[512,6,512]{0,2,1:T(8,128)(2,1)} %bitcast.124), kind=kOutput, calls=%fused_computation.31 | convolution fusion | flops 1613496320 | bytes 13631488 | tf_op jit(solution)/shard_map/kba,bkc->kac/dot_general | solution.py:33
  166.8 4.0 %fusion.18 = bf16[6,512,512]{2,1,0:T(8,128)(2,1)} fusion(bf16[6,512,512]{2,1,0:T(8,128)(2,1)S(1)} %add_convert_fusion.1, f32[6,512,512]{2,1,0:T(8,128)S(1)} %bitcast.123, f32[512,512]{1,0:T(8,128)S(1)} %fusion.20), kind=kOutput, calls=%fused_computation.40 | convolution fusion | flops 1615331328 | bytes 13631488 | tf_op jit(solution)/shard_map/kab,kbc->akc/dot_general | solution.py:41
  170.8 4.5 %fusion.15 = f32[512,512]{1,0:T(8,128)S(1)} fusion(bf16[3072,512]{1,0:T(8,128)(2,1)S(1)} %copy-done, s32[]{:T(128)S(6)} %select_n.19, bf16[512,3072]{0,1:T(8,128)(2,1)} %bitcast.126), kind=kOutput, calls=%fused_computation.37 | convolution fusion | flops 1610612736 | bytes 7340036 | tf_op jit(solution)/shard_map/dot_general | solution.py:48
  177.6 101.0 %all-reduce.4.cloned.1.call-done = f32[512,2,512]{2,1,0:T(2,128)} async-done(((f32[512,2,512]{2,1,0:T(2,128)}), f32[512,2,512]{2,1,0:T(2,128)}) %all-reduce.4.cloned.1.call-update) | async-done | bytes 2097168 | tf_op jit(solution)/shard_map/psum | solution.py:71
  (74 shorter events, 34.3 us)
Async XLA Ops:
  6.5 142.5 %all-gather.2.cloned.1.call-start = ((), (), s32[]{:S(2)}) async-start(), calls=%async_computation | async-start | bytes 1114112 | tf_op jit(solution)/shard_map/all_gather | solution.py:65
  8.1 270.5 %all-reduce.4.cloned.1.call-start = ((), (), s32[]{:S(2)}) async-start(), calls=%async_computation.1 | async-start | bytes 4194304 | tf_op jit(solution)/shard_map/psum | solution.py:71
  10.2 7.5 %copy-start.3 = (bf16[6,15]{1,0:T(8,128)(2,1)S(1)}, bf16[6,15]{1,0:T(8,128)(2,1)}, u32[]{:S(2)}) copy-start(bf16[6,15]{1,0:T(8,128)(2,1)} %param.15) | copy-start | bytes 544
  59.2 15.3 %copy-start.5 = (f32[1,6,8,8]{3,2,1,0:T(8,128)S(1)}, f32[1,6,8,8]{3,2,1,0:T(8,128)}, u32[]{:S(2)}) copy-start(f32[1,6,8,8]{3,2,1,0:T(8,128)} %param.11) | copy-start | bytes 4612
  125.3 12.9 %copy-start.4 = (bf16[6,15]{1,0:T(8,128)(2,1)S(1)}, bf16[6,15]{1,0:T(8,128)(2,1)}, u32[]{:S(2)}) copy-start(bf16[6,15]{1,0:T(8,128)(2,1)} %param.14) | copy-start | bytes 544
  160.3 6.5 %slice-start = ((s8[6291456]{0:T(1024)(128)(4,1)}), s8[4194304]{0:T(1024)(128)(4,1)S(1)}, s32[]{:S(2)}) async-start(s8[6291456]{0:T(1024)(128)(4,1)} %bitcast.122), calls=%async_computation.2 | async-start | bytes 8388608
  160.3 6.2 %copy-start.1 = (s32[1,512,512]{2,1,0:T(8,128)S(1)}, s32[1,512,512]{2,1,0:T(8,128)}, u32[]{:S(2)}) copy-start(s32[1,512,512]{2,1,0:T(8,128)} %param.10) | copy-start | bytes 3145732
  160.3 6.2 %copy-start.2 = (bf16[1,512,512]{2,1,0:T(8,128)(2,1)S(1)}, bf16[1,512,512]{2,1,0:T(8,128)(2,1)}, u32[]{:S(2)}) copy-start(bf16[1,512,512]{2,1,0:T(8,128)(2,1)} %param.9) | copy-start | bytes 1572868
  160.3 6.5 %slice-start.1 = ((s8[6291456]{0:T(1024)(128)(4,1)}), s8[2097152]{0:T(1024)(128)(4,1)S(1)}, s32[]{:S(2)}) async-start(s8[6291456]{0:T(1024)(128)(4,1)} %bitcast.122), calls=%async_computation.3 | async-start | bytes 4194304
  166.8 4.0 %copy-start = (bf16[3072,512]{1,0:T(8,128)(2,1)S(1)}, bf16[3072,512]{1,0:T(8,128)(2,1)}, u32[]{:S(2)}) copy-start(bf16[3072,512]{1,0:T(8,128)(2,1)} %fusion.1) | copy-start | bytes 9437188
Sparse Core Ops, SparseCore 0:
  9.5 40.5 all-gather.1
  177.7 100.8 all-reduce.3
where the time goes:
time: 289 us; the launch traced here: 287 us
  local copies, waits for them, and re-layouts  101 us (35%)
  waiting for transfers between devices  101 us (35%)
  other arithmetic  50.1 us (17%)
  matrix products  18.5 us (6%)
  between operations  16.4 us (6%)
    psum x1, waiting for transfers between devices, per_device(): lax.psum(back_rows(padded_back, back_stack, row_shift, patch_index, patch...  101 us
    convert_element_type x30, local copies, waits for them, and re-layouts, band_stack(): matches = ((offset == tap_index) & inside).astype(jnp.float32)  70.9 us
    convert_element_type x3, other arithmetic, band_stack(): return running.astype(jnp.bfloat16)  31.8 us
    convert_element_type x2, other arithmetic, band_stack(): matches = ((offset == tap_index) & inside).astype(jnp.float32)  14.4 us
    reshape x1, local copies, waits for them, and re-layouts, exposure_back(): mix_full = jnp.broadcast_to(blur_weights[:, :, None, :, None], (basis_cou...  11.5 us
    dynamic_slice x2, local copies, waits for them, and re-layouts, exposure_back(): lax.dynamic_slice_in_dim(padded, DMAX + row_shift, extent, 0)  7.27 us
    dot_general x1, matrix products, exposure_back(): jnp.einsum('kba,bkc->kac', column_band, shifted, preferred_element_type=j...  6.17 us
  transfers between devices with their start and end apart: 2, of which 1 were waited for; matrix products, arithmetic and copies ran while one was open for 48% of the time, Pallas kernels for 0%

commit v1 on v0

--- a/solution.py
+++ b/solution.py
@@ -68,9 +68,9 @@
     padded_back = exposure_back(
         rowed, observed[0], pixel_mask[0], blur_mix[0], row_shift, column_band
     )
-    complete = lax.psum(
-        back_rows(padded_back, back_stack, row_shift, patch_index, patch_count, 0, extent), "exp"
-    )
+    x = back_rows(padded_back, back_stack, row_shift, patch_index, patch_count, 0, extent)
+    blocks = lax.all_gather(x, "exp")
+    complete = jnp.sum(blocks, axis=0)
     return lax.dynamic_slice_in_dim(complete, lax.axis_index("exp") * band_rows, band_rows, 0)
 
 

time: 289 us -> 370 us (1.28)
  waiting for transfers between devices: 101 us -> 171 us
  other arithmetic: 50.1 us -> 62.2 us
    all_gather x0 -> x1, waiting for transfers between devices: none -> 171 us  [per_device(): blocks = lax.all_gather(x, 'exp')]
    psum x1 -> x0, waiting for transfers between devices: 101 us -> none  [per_device(): lax.psum(back_rows(padded_back, back_stack, row_shift, patch_index, patch...]
    reduce_sum x0 -> x1, other arithmetic: none -> 12.7 us  [per_device(): complete = jnp.sum(blocks, axis=0)]
  transfers between devices with their start and end apart: 2 -> 2, of which waited for: 1 -> 1; matrix products, arithmetic and copies ran while one was open for 48% -> 37% of each run, Pallas kernels for 0% -> 0%
where the time goes in v1:
time: 370 us; the launch traced here: 368 us
  waiting for transfers between devices  171 us (46%)
  local copies, waits for them, and re-layouts  100 us (27%)
  other arithmetic  62.2 us (17%)
  matrix products  18.5 us (5%)
  between operations  16.5 us (4%)
    all_gather x1, waiting for transfers between devices, per_device(): blocks = lax.all_gather(x, 'exp')  171 us
    convert_element_type x30, local copies, waits for them, and re-layouts, band_stack(): matches = ((offset == tap_index) & inside).astype(jnp.float32)  70.9 us
    convert_element_type x3, other arithmetic, band_stack(): return running.astype(jnp.bfloat16)  31.8 us
    convert_element_type x2, other arithmetic, band_stack(): matches = ((offset == tap_index) & inside).astype(jnp.float32)  14.4 us
    reduce_sum x1, other arithmetic, per_device(): complete = jnp.sum(blocks, axis=0)  12.7 us
    reshape x1, local copies, waits for them, and re-layouts, exposure_back(): mix_full = jnp.broadcast_to(blur_weights[:, :, None, :, None], (basis_cou...  11.5 us
  transfers between devices with their start and end apart: 2, of which 1 were waited for; matrix products, arithmetic and copies ran while one was open for 37% of the time, Pallas kernels for 0%

profile of v1, /device:TPU:0, one launch (start us, length us, event | category | flops | bytes accessed | tf_op | source)
XLA Modules:
  0.0 368.2 jit_solution(5421199459017871329)
XLA Ops:
  10.3 7.4 %fusion.68 = (f32[512,512]{0,1:T(8,128)S(1)}, f32[512,512]{0,1:T(8,128)}, f32[512,512]{0,1:T(8,128)S(1)}, f32[512,512]{0,1:T(8,128)S(1)}, f32[512,512]{0,1:T(8,1...) fusion(s32[]{:T(128)} %bitcast.3, ...), kind=kLoop, calls=%fused_computation.95 | loop fusion | flops 25165824 | bytes 31457796 | tf_op jit(solution)/shard_map/convert_element_type | solution.py:17
  18.0 8.4 %add_convert_fusion = bf16[512,6,512]{0,2,1:T(8,128)(2,1)} fusion(f32[512,512]{0,1:T(8,128)S(1)} %get-tuple-element.51, f32[6]{0:T(128)S(1)} %get-tuple-element.33, f32[512,512]{0,1:T(8,128)S(1)} %get-tuple-element.52, f32[6]{0:T(128)S(1)} %get-tuple-element.34, f32[512,512]{0,1:T(8,128)S(1)} %get-tuple-element.53, f32[6]{0:T(128)S(1)} %get-tuple-element.21, ...), kind=kLoop, calls=%fused_computation.32 | loop fusion | flops 47185920 | bytes 18874728 | tf_op jit(solution)/shard_map/convert_element_type | solution.py:21
  26.4 7.0 %fusion.128 = (f32[512,512]{0,1:T(8,128)}, f32[512,512]{0,1:T(8,128)}, f32[512,512]{0,1:T(8,128)}, f32[512,512]{0,1:T(8,128)}, f32[512,512]{0,1:T(8,128)}, /*ind...) fusion(pred[512]{0:T(512)(128)(4,1)S(1)} %iota_compare_fusion), kind=kLoop, calls=%fused_computation.155 | loop fusion | flops 12320768 | bytes 15729152 | tf_op jit(solution)/shard_map/convert_element_type | solution.py:17
  38.8 2.6 copy.82
  44.0 2.6 copy.84
  46.5 2.5 copy.85
  51.6 2.6 copy.87
  54.1 2.5 copy.88
  56.7 2.6 copy.89
  61.8 2.5 copy.91
  64.3 2.6 copy.92
  66.9 2.6 copy.93
  69.5 2.5 copy.94
  72.0 2.5 copy.95
  74.5 5.4 %broadcast_in_dim.19 = f32[6,8,64,8,64]{4,3,2,1,0:T(8,128)} broadcast(f32[6,8,8]{2,1,0:T(8,128)S(1)} %bitcast.127), dimensions={0,1,3} | broadcast | bytes 6292992 | tf_op jit(solution)/shard_map/broadcast_in_dim | solution.py:34
  80.0 11.5 %reshape.1300 = f32[6,512,512]{2,1,0:T(8,128)} reshape(f32[6,8,64,8,64]{4,3,2,1,0:T(8,128)} %broadcast_in_dim.19) | data formatting | bytes 12582912 | tf_op jit(solution)/shard_map/reshape | solution.py:37
  91.5 2.5 copy.101
  94.1 2.6 copy.102
  101.7 2.6 copy.105
  104.3 2.6 copy.106
  106.8 2.6 copy.107
  117.0 2.6 copy.111
  119.6 2.5 copy.112
  125.3 12.8 %fusion.1 = bf16[3072,512]{1,0:T(8,128)(2,1)} fusion(f32[512,512]{1,0:T(8,128)S(1)} %copy.115, f32[3072]{0:T(1024)S(1)} %mul.935, f32[512,512]{1,0:T(8,128)S(1)} %copy.114, f32[3072]{0:T(1024)S(1)} %mul.929, f32[512,512]{1,0:T(8,128)} %copy.113, f32[3072]{0:T(1024)S(1)} %mul.923, f32[512,512]{1,0:T(8,128)} %copy.112, f32[3072]{0:T(1024)S(1)} %mul.917, ...), kind=kLoop, calls=%fused_computation.2 | loop fusion | flops 47185920 | bytes 19058688 | tf_op jit(solution)/shard_map/convert_element_type | solution.py:21
  138.5 10.5 %add_convert_fusion.1 = bf16[6,512,512]{2,1,0:T(8,128)(2,1)S(1)} fusion(f32[512,512]{1,0:T(8,128)} %copy.95, f32[6]{0:T(128)S(1)} %get-tuple-element.18, f32[512,512]{1,0:T(8,128)} %copy.94, f32[6]{0:T(128)S(1)} %get-tuple-element.19, f32[512,512]{1,0:T(8,128)} %copy.93, f32[6]{0:T(128)S(1)} %get-tuple-element.6, f32[512,512]{1,0:T(8,128)} %copy.92, ...), kind=kLoop, calls=%fused_computation.33 | loop fusion | flops 47185920 | bytes 18874728 | tf_op jit(solution)/shard_map/convert_element_type | solution.py:21
  149.1 3.9 %convolution_convert_fusion = bf16[512,3072]{1,0:T(8,128)(2,1)S(1)} fusion(bf16[512,3072]{0,1:T(8,128)(2,1)} %bitcast.125, bf16[512,2,512]{2,0,1:T(8,128)(2,1)} %all-gather.3.cloned.1.call-done, s32[]{:T(128)S(6)} %select_n.24), kind=kOutput, calls=%fused_computation.34 | convolution fusion | flops 1612185600 | bytes 6815748 | tf_op jit(solution)/shard_map/dot_general | solution.py:67
  155.5 4.7 %copy.97 = bf16[512,3072]{0,1:T(8,128)(2,1)} copy(bf16[512,3072]{1,0:T(8,128)(2,1)} %pad_dynamic-slice_fusion.1) | data formatting | bytes 6291456 | tf_op jit(solution)/shard_map/dynamic_slice | solution.py:30
  160.3 6.2 %multiply_reduce_fusion = f32[512,512]{1,0:T(8,128)S(1)} fusion(f32[6,512,512]{2,1,0:T(8,128)} %reshape.1300, bf16[6,512,512]{2,1,0:T(8,128)(2,1)S(1)} %add_convert_fusion.1, bf16[512,6,512]{0,2,1:T(8,128)(2,1)} %bitcast.124), kind=kOutput, calls=%fused_computation.31 | convolution fusion | flops 1613496320 | bytes 13631488 | tf_op jit(solution)/shard_map/kba,bkc->kac/dot_general | solution.py:33
  166.8 4.0 %fusion.18 = bf16[6,512,512]{2,1,0:T(8,128)(2,1)} fusion(bf16[6,512,512]{2,1,0:T(8,128)(2,1)S(1)} %add_convert_fusion.1, f32[6,512,512]{2,1,0:T(8,128)S(1)} %bitcast.123, f32[512,512]{1,0:T(8,128)S(1)} %fusion.20), kind=kOutput, calls=%fused_computation.40 | convolution fusion | flops 1615331328 | bytes 13631488 | tf_op jit(solution)/shard_map/kab,kbc->akc/dot_general | solution.py:41
  170.8 4.5 %fusion.15 = f32[512,512]{1,0:T(8,128)S(1)} fusion(bf16[3072,512]{1,0:T(8,128)(2,1)S(1)} %copy-done, s32[]{:T(128)S(6)} %select_n.26, bf16[512,3072]{0,1:T(8,128)(2,1)} %bitcast.126), kind=kOutput, calls=%fused_computation.37 | convolution fusion | flops 1610612736 | bytes 7340036 | tf_op jit(solution)/shard_map/dot_general | solution.py:48
  177.0 170.9 %all-gather.5.cloned.1.call-done = f32[16,512,2,512]{3,1,2,0:T(8,128)} async-done(((f32[1,512,2,512]{3,1,2,0:T(8,128)}), f32[16,512,2,512]{3,1,2,0:T(8,128)}) %all-gather.5.cloned.1.call-update) | async-done | bytes 33554448 | tf_op jit(solution)/shard_map/all_gather | solution.py:72
  347.9 12.7 %reduce_sum.22 = f32[512,2,512]{2,0,1:T(8,128)S(1)} reduce(f32[16,512,2,512]{3,1,2,0:T(8,128)} %all-gather.5.cloned.1.call-done, f32[]{:T(128)} %constant.56.clone.1), dimensions={0}, to_apply=%region_1.2 | reduce | flops 7864320 | bytes 35651588 | tf_op jit(solution)/shard_map/reduce_sum | solution.py:73
  (76 shorter events, 35.5 us)
Async XLA Ops:
  6.5 142.5 %all-gather.3.cloned.1.call-start = ((), (), s32[]{:S(2)}) async-start(), calls=%async_computation | async-start | bytes 1114112 | tf_op jit(solution)/shard_map/all_gather | solution.py:65
  8.1 339.7 %all-gather.5.cloned.1.call-start = ((), (), s32[]{:S(2)}) async-start(), calls=%async_computation.1 | async-start | bytes 35651584 | tf_op jit(solution)/shard_map/all_gather | solution.py:72
  10.2 7.5 %copy-start.3 = (bf16[6,15]{1,0:T(8,128)(2,1)S(1)}, bf16[6,15]{1,0:T(8,128)(2,1)}, u32[]{:S(2)}) copy-start(bf16[6,15]{1,0:T(8,128)(2,1)} %param.15) | copy-start | bytes 544
  59.2 15.3 %copy-start.5 = (f32[1,6,8,8]{3,2,1,0:T(8,128)S(1)}, f32[1,6,8,8]{3,2,1,0:T(8,128)}, u32[]{:S(2)}) copy-start(f32[1,6,8,8]{3,2,1,0:T(8,128)} %param.11) | copy-start | bytes 4612
  125.3 12.9 %copy-start.4 = (bf16[6,15]{1,0:T(8,128)(2,1)S(1)}, bf16[6,15]{1,0:T(8,128)(2,1)}, u32[]{:S(2)}) copy-start(bf16[6,15]{1,0:T(8,128)(2,1)} %param.14) | copy-start | bytes 544
  160.3 6.5 %slice-start = ((s8[6291456]{0:T(1024)(128)(4,1)}), s8[4194304]{0:T(1024)(128)(4,1)S(1)}, s32[]{:S(2)}) async-start(s8[6291456]{0:T(1024)(128)(4,1)} %bitcast.122), calls=%async_computation.2 | async-start | bytes 8388608
  160.3 6.2 %copy-start.1 = (s32[1,512,512]{2,1,0:T(8,128)S(1)}, s32[1,512,512]{2,1,0:T(8,128)}, u32[]{:S(2)}) copy-start(s32[1,512,512]{2,1,0:T(8,128)} %param.10) | copy-start | bytes 3145732
  160.3 6.2 %copy-start.2 = (bf16[1,512,512]{2,1,0:T(8,128)(2,1)S(1)}, bf16[1,512,512]{2,1,0:T(8,128)(2,1)}, u32[]{:S(2)}) copy-start(bf16[1,512,512]{2,1,0:T(8,128)(2,1)} %param.9) | copy-start | bytes 1572868
  160.3 6.5 %slice-start.1 = ((s8[6291456]{0:T(1024)(128)(4,1)}), s8[2097152]{0:T(1024)(128)(4,1)S(1)}, s32[]{:S(2)}) async-start(s8[6291456]{0:T(1024)(128)(4,1)} %bitcast.122), calls=%async_computation.3 | async-start | bytes 4194304
  166.8 4.0 %copy-start = (bf16[3072,512]{1,0:T(8,128)(2,1)S(1)}, bf16[3072,512]{1,0:T(8,128)(2,1)}, u32[]{:S(2)}) copy-start(bf16[3072,512]{1,0:T(8,128)(2,1)} %fusion.1) | copy-start | bytes 9437188
Sparse Core Ops, SparseCore 0:
  9.5 40.5 all-gather.2
  177.1 170.7 all-gather.4
